TPU v7x, 256 devices: a whole 4x4x8 slice. The times are simulated.
256 devices in a mesh: gx: 16 (over y_lo, x, core), ch: 16 (over z, y_hi).
Axes of the slice: x: 4, y: 4 (y_hi: 2, y_lo: 2; y = y_hi * 2 + y_lo), z: 8, core: 2. Of those that a mesh axis runs over, the one named last changes fastest.
Arguments:
- activations: bfloat16 [128, 256, 4, 128], P('ch', 'gx'), may hold values from -6 to 6
- conv_weight: bfloat16 [27, 128, 128], P(None, None, 'ch'), may hold values from -0.109375 to 0.109375
- out_grad: bfloat16 [128, 256, 4, 128], P('ch', 'gx'), may hold values from -6 to 6
Outputs:
- features_out: bfloat16 [128, 256, 4, 128], P('ch', 'gx')
- input_grad: bfloat16 [128, 256, 4, 128], P('ch', 'gx')
All inputs are finite; a program needn't handle non-finite values.
Results may differ from a plain program's by a relative error of at most 0.001.
Values may be sent and summed in bfloat16 or wider, within the bound.
No kernel may reach another device: no remote copies, remote signals or barrier semaphores. Data moves between devices by JAX's collectives and lax.ppermute only.
A program may use at most 64 MiB of HBM per device.

v0:
```python
import functools

import jax
import jax.numpy as jnp
from jax import lax
from jax.experimental import pallas as pl
from jax.experimental.pallas import tpu as pltpu
from jax.sharding import PartitionSpec as P


VMEM = pl.BlockSpec(memory_space=pltpu.VMEM)
HBM = pl.BlockSpec(memory_space=pltpu.HBM)
PARAMS = pltpu.CompilerParams(vmem_limit_bytes=16 * 2**20)
F32 = jnp.float32
BF16 = jnp.bfloat16


def lanes(shape):
    return lax.broadcasted_iota(jnp.int32, shape, len(shape) - 1)


def pair_of(level, core, count):
    return level + core * (count // 2 - 1 - 2 * level)


def quarter(taps, index):
    size = (taps + 3) // 4
    return (min(index * size, taps - size) if isinstance(index, int) else jnp.minimum(index * size, taps - size)), size


def both(first, second):
    size = first.shape[-1]
    early = lanes(first.shape) < size // 2
    turned_first, turned_second = (pltpu.roll(x, size // 2, x.ndim - 1) for x in (first, second))
    return jnp.where(early, first, turned_second), jnp.where(early, turned_first, second)


def pack_kernel(act_hbm, grad_hbm, weight_hbm, send_ref, act_ref, grad_ref, weight_ref, rows_ref, sems):
    copies = [
        pltpu.make_async_copy(source, target, sems.at[at])
        for at, (source, target) in enumerate(
            ((act_hbm, act_ref), (grad_hbm, grad_ref), (weight_hbm, weight_ref))
        )
    ]
    for copy in copies:
        copy.start()
    core = lax.rem(lax.axis_index("gx"), 2)
    count, (rows, _, depth, height) = send_ref.shape[0], act_ref.shape
    taps, _, fan = weight_ref.shape
    block = rows * depth
    side = height // 2
    copies[0].wait()
    copies[1].wait()
    lane = lanes((rows, height))
    for level in range(count // 2):
        pair = pair_of(level, core, count)
        edges = [jnp.zeros((rows, height), F32) for _ in range(2)]
        for plane in range(2):
            maps = []
            for tensor, ref in enumerate((act_ref, grad_ref)):
                values = ref[:, 2 * pair + plane].reshape(block, height).astype(F32)
                maps.append(values)
                rows_ref[...] = values
                for z in range(depth):
                    column = rows_ref[pl.ds(z, rows, stride=depth), :]
                    spot = side * plane + 8 * tensor + z
                    for half in range(2):
                        edge = side - half
                        turned = pltpu.roll(column, (spot - edge) % height, 1)
                        edges[half] = jnp.where(lane == spot, turned, edges[half])
            start = plane * (block + rows)
            for half, values in enumerate(both(*maps)):
                send_ref[2 * level + half, start : start + block, :] = values.astype(BF16)
        for half in range(2):
            send_ref[2 * level + half, block : block + rows, :] = edges[half].astype(BF16)
    copies[2].wait()
    first, shared = quarter(taps, lax.rem(lax.axis_index("gx"), 4))
    filters = weight_ref[pl.ds(first, shared)].reshape(shared * rows, fan)
    for chip in range(count):
        send_ref[chip, 2 * block + rows :, :] = filters


def prepare_kernel(own_ref, core_ref, x_ref, diagonal_ref, forward_ref, backward_ref, filters_ref, *, taps):
    count, _, channels = own_ref.shape
    rows = channels // count
    mine = lax.rem(lax.axis_index("gx"), 4)
    core, x = lax.rem(mine, 2), mine // 2
    for at, ref in ((2 * x + core, own_ref), (2 * x + 1 - core, core_ref),
                    (2 - 2 * x + core, x_ref), (3 - 2 * x - core, diagonal_ref)):
        filters_ref[at] = ref[...]

    def spot(index):
        return slice(index * channels, (index + 1) * channels)

    for a in range(3):
        for b in range(3):
            for c in range(3):
                tap = 9 * a + 3 * b + c
                part = tap // quarter(taps, 0)[1]
                at = tap - quarter(taps, part)[0]
                matrix = filters_ref[part, :, at * rows : (at + 1) * rows, :].reshape(channels, channels)
                forward_ref[spot(b), spot(3 * c + a)] = matrix
                backward_ref[spot(b), spot(3 * c + a)] = matrix.T


def conv_kernel(own_ref, low_ref, high_ref, forward_ref, backward_ref, send_ref, cells_ref, wide_ref, *, depth):
    count, span, height = own_ref.shape
    rows = span // (2 * depth + 1)
    block = rows * depth
    channels = count * rows
    side = height // 2
    right = lax.rem(lax.axis_index("ch"), 2)

    def spot(index):
        return slice(index * channels, (index + 1) * channels)

    lane = lanes((channels, height))
    early = lane < side
    within = lane % side

    def edge_of(ref, start):
        return ref[:, start : start + rows, :].astype(F32).reshape(channels, height)

    own_edge, low_edge, high_edge = edge_of(own_ref, block), edge_of(low_ref, 0), edge_of(high_ref, block)
    edges = (
        pltpu.roll(jnp.where(early, own_edge, low_edge), side, 1),
        own_edge,
        pltpu.roll(jnp.where(early, high_edge, own_edge), side, 1),
    )
    planes = (
        low_ref[:, rows : rows + block, :],
        own_ref[:, 0:block, :],
        own_ref[:, block + rows : 2 * block + rows, :],
        high_ref[:, 0:block, :],
    )
    for at, values in enumerate(planes):
        wide_ref[at] = values.astype(F32).reshape(channels * depth, height)

    for c in range(3):
        for tensor in range(2):
            direction = 1 - 2 * tensor
            outside = 0 if direction * (c - 1) < 0 else depth - 1
            if c != 1:
                cells_ref[tensor, 3 * c * channels : 3 * (c + 1) * channels, outside * height : (outside + 1) * height] = (
                    jnp.zeros((3 * channels, height), BF16)
                )
            for a in range(3):
                edge = edges[1 + direction * (a - 1)]
                shift = 8 * tensor + direction * (c - 1)
                source = within + direction * (c - 1)
                inside = (within < depth) & (source >= 0) & (source < depth)
                moved = pltpu.roll(edge, -shift % height, 1)
                cells_ref[tensor, spot(3 * c + a), depth * height :] = jnp.where(inside, moved, 0.0).astype(BF16)
    for z in range(depth):
        pieces = [wide_ref[at, pl.ds(z, channels, stride=depth), :] for at in range(4)]
        for step in range(3):
            for tensor, values in enumerate(both_planes(pieces[step], pieces[step + 1], early, side)):
                direction = 1 - 2 * tensor
                a = 1 + direction * (step - 1)
                values = values.astype(BF16)
                for c in range(3):
                    target = z - direction * (c - 1)
                    if 0 <= target < depth:
                        cells_ref[tensor, spot(3 * c + a), target * height : (target + 1) * height] = values

    for tensor in range(2):
        direction = 1 - 2 * tensor
        filters = (forward_ref, backward_ref)[tensor][...]
        sums = jnp.dot(filters, cells_ref[tensor], preferred_element_type=F32)
        beyond = sums[:, depth * height :]
        beyond = jnp.where(right == 1, beyond[spot(1 - direction)], beyond[spot(1 + direction)])
        border = jnp.where(right == 1, 0, side - 1)
        for z in range(depth):
            columns = slice(z * height, (z + 1) * height)
            before, middle, after = (sums[spot(b), columns] for b in (1 - direction, 1, 1 + direction))
            before = jnp.where(within == 0, 0.0, pltpu.roll(before, 1, 1))
            after = jnp.where(within == side - 1, 0.0, pltpu.roll(after, height - 1, 1))
            extra = jnp.where(within == border, pltpu.roll(beyond, border + (height - z), 1), 0.0)
            wide_ref[tensor, pl.ds(z, channels, stride=depth), :] = before + middle + after + extra
        result = wide_ref[tensor].astype(BF16).reshape(count, block, height)
        send_ref[:, tensor * block : (tensor + 1) * block, :] = result


def both_planes(first, second, early, side):
    turned_first, turned_second = pltpu.roll(first, side, 1), pltpu.roll(second, side, 1)
    return jnp.where(early, first, turned_second), jnp.where(early, turned_first, second)


def unpack_kernel(got_ref, features_ref, gradient_ref):
    core = lax.rem(lax.axis_index("gx"), 2)
    count, _, height = got_ref.shape
    rows, _, depth, _ = features_ref.shape
    block = rows * depth
    for level in range(count // 2):
        pair = pair_of(level, core, count)
        for tensor, ref in enumerate((features_ref, gradient_ref)):
            start = tensor * block
            halves = [got_ref[2 * level + side, start : start + block, :].astype(F32) for side in range(2)]
            for plane, values in enumerate(both(*halves)):
                ref[:, 2 * pair + plane] = values.astype(BF16).reshape(rows, depth, height)


def local(slabs, count, activations, conv_weight, out_grad):
    rows, _, depth, height = activations.shape
    taps, channels, _ = conv_weight.shape
    block = rows * depth
    span = 2 * block + rows
    shared = quarter(taps, 0)[1]
    pairs = count // 2
    send = pl.pallas_call(
        pack_kernel,
        out_shape=jax.ShapeDtypeStruct((count, span + shared * rows, height), BF16),
        in_specs=[HBM, HBM, HBM],
        out_specs=VMEM,
        scratch_shapes=[
            pltpu.VMEM(activations.shape, BF16),
            pltpu.VMEM(out_grad.shape, BF16),
            pltpu.VMEM((taps, rows, channels), BF16),
            pltpu.VMEM((block, height), F32),
            pltpu.SemaphoreType.DMA((3,)),
        ],
        compiler_params=PARAMS,
        name="pack",
    )(*(pltpu.with_memory_space_constraint(x, pltpu.HBM) for x in (activations, out_grad, jnp.swapaxes(conv_weight, 1, 2))))
    got = lax.all_to_all(send, "ch", 0, 0, tiled=True)
    own, own_filters = got[:, :span], got[:, span:]
    across_core, across_x = ([(slab, slab ^ step) for slab in range(slabs)] for step in (1, 2))
    x_filters = lax.ppermute(own_filters, "gx", across_x)
    core_filters = lax.ppermute(own_filters, "gx", across_core)
    diagonal_filters = lax.ppermute(x_filters, "gx", across_core)
    ring = []
    for side in range(2):
        order = [
            slab * count + 2 * pair_of(pair, slab % 2, count) + side for slab in range(slabs) for pair in range(pairs)
        ]
        ring += zip(order, order[1:] + order[:1])
    low = lax.ppermute(got[:, block:span], ("gx", "ch"), ring)
    high = lax.ppermute(got[:, : block + rows], ("gx", "ch"), [(to, at) for at, to in ring])
    forward, backward = pl.pallas_call(
        functools.partial(prepare_kernel, taps=taps),
        out_shape=[jax.ShapeDtypeStruct((3 * channels, 9 * channels), BF16)] * 2,
        in_specs=[VMEM, VMEM, VMEM, VMEM],
        out_specs=[VMEM, VMEM],
        scratch_shapes=[pltpu.VMEM((4, count, shared * rows, channels), BF16)],
        cost_estimate=pl.CostEstimate(flops=0, bytes_accessed=4 * 2**20, transcendentals=0),
        compiler_params=PARAMS,
        name="prepare",
    )(own_filters, core_filters, x_filters, diagonal_filters)
    result = pl.pallas_call(
        functools.partial(conv_kernel, depth=depth),
        out_shape=jax.ShapeDtypeStruct((count, 2 * block, height), BF16),
        in_specs=[VMEM, VMEM, VMEM, VMEM, VMEM],
        out_specs=VMEM,
        scratch_shapes=[
            pltpu.VMEM((2, 9 * channels, (depth + 1) * height), BF16),
            pltpu.VMEM((4, channels * depth, height), F32),
        ],
        compiler_params=PARAMS,
        name="conv",
    )(own, low, high, forward, backward)
    back = lax.all_to_all(result, "ch", 0, 0, tiled=True)
    return pl.pallas_call(
        unpack_kernel,
        out_shape=(jax.ShapeDtypeStruct(activations.shape, BF16), jax.ShapeDtypeStruct(out_grad.shape, BF16)),
        in_specs=[VMEM],
        out_specs=(VMEM, VMEM),
        compiler_params=PARAMS,
        name="unpack",
    )(back)


def solution(mesh):
    return jax.shard_map(
        functools.partial(local, mesh.shape["gx"], mesh.shape["ch"]),
        mesh=mesh,
        in_specs=(P("ch", "gx", None, None), P(None, None, "ch"), P("ch", "gx", None, None)),
        out_specs=(P("ch", "gx", None, None), P("ch", "gx", None, None)),
        check_vma=False,
    )
```

profile of v0, /device:TPU:2, one launch (start us, length us, event | category | flops | bytes accessed | tf_op | source)
XLA Modules:
  0.0 67.3 jit_solution(3044511388935836795)
XLA Ops:
  0.6 1.4 %pack.1 = bf16[16,128,128]{2,1,0:T(8,128)(2,1)S(1)} custom-call(bf16[8,16,4,128]{3,2,1,0:T(4,128)(2,1)} %act_hbm.1, bf16[8,16,4,128]{3,2,1,0:T(4,128)(2,1)} %grad_hbm.1, bf16[27,8,128]{2,1,0:T(8,128)(2,1)} %bitcast.1), custom_call_target="tpu_custom_call" | custom-call | tf_op jit(solution)/shard_map/pack/pallas_call | solution.py:210
  2.0 29.8 %all_to_all.10 = bf16[16,128,128]{2,1,0:T(8,128)(2,1)S(1)} all-to-all(bf16[16,128,128]{2,1,0:T(8,128)(2,1)S(1)} %pack.1), channel_id=1, replica_groups=mesh['gx'=16,'ch'=16] {'ch'}, dimensions={0} | all-to-all | bytes 1048576 | tf_op jit(solution)/shard_map/all_to_all | solution.py:225
  31.9 0.6 collective-permute-start.3
  32.5 0.0 collective-permute-start.2
  32.5 5.5 %collective-permute-done.3.x_ref = bf16[16,56,128]{2,1,0:T(8,128)(2,1)S(1)} collective-permute-done((bf16[16,56,128]{2,1,0:T(8,128)(2,1)S(1)}, bf16[16,56,128]{2,1,0:T(8,128)(2,1)S(1)}, u32[]{:S(2)}, u32[]{:S(2)}) %collective-permute-start.3) | collective-permute-done | bytes 229408 | tf_op jit(solution)/shard_map/ppermute | solution.py:228
  38.0 0.0 collective-permute-start.4
  38.0 0.1 collective-permute-start
  38.1 1.7 %collective-permute-start.1 = (bf16[16,40,128]{2,1,0:T(8,128)(2,1)S(1)}, bf16[16,40,128]{2,1,0:T(8,128)(2,1)S(1)}, u32[]{:S(2)}, u32[]{:S(2)}) collective-permute-start(bf16[16,40,128]{2,1,0:T(8,128)(2,1)S(1)} %get-tuple-element.6), channel_id=1, source_target_pairs={{2,0},{4,2},{6,4},{8,6},{10,8},{12,10},{14,12},{30,14},{28,30},{26... | collective-permute-start | bytes 491528 | tf_op jit(solution)/shard_map/ppermute | solution.py:238
  39.9 0.0 collective-permute-done.2.core_ref
  39.9 0.0 collective-permute-done.4.diagonal_ref
  39.9 0.4 prepare.1
  40.3 2.5 %collective-permute-done.low_ref = bf16[16,40,128]{2,1,0:T(8,128)(2,1)S(1)} collective-permute-done((bf16[16,40,128]{2,1,0:T(8,128)(2,1)S(1)}, bf16[16,40,128]{2,1,0:T(8,128)(2,1)S(1)}, u32[]{:S(2)}, u32[]{:S(2)}) %collective-permute-start) | collective-permute-done | bytes 163872 | tf_op jit(solution)/shard_map/ppermute | solution.py:237
  42.8 1.9 %collective-permute-done.1.high_ref = bf16[16,40,128]{2,1,0:T(8,128)(2,1)S(1)} collective-permute-done((bf16[16,40,128]{2,1,0:T(8,128)(2,1)S(1)}, bf16[16,40,128]{2,1,0:T(8,128)(2,1)S(1)}, u32[]{:S(2)}, u32[]{:S(2)}) %collective-permute-start.1) | collective-permute-done | bytes 163872 | tf_op jit(solution)/shard_map/ppermute | solution.py:238
  44.7 2.1 %conv.1 = bf16[16,64,128]{2,1,0:T(8,128)(2,1)S(1)} custom-call(bf16[16,72,128]{2,1,0:T(8,128)(2,1)S(1)} %slice.16.own_ref, bf16[16,40,128]{2,1,0:T(8,128)(2,1)S(1)} %collective-permute-done.low_ref, bf16[16,40,128]{2,1,0:T(8,128)(2,1)S(1)} %collective-permute-done.1.high_ref, bf16[384,1152]{1,0:T(8,128)(2,1)S(1)} %get-tuple-element.4.forward_ref, ...), custom_call_target="tpu_custom_call" | custom-call | tf_op jit(solution)/shard_map/conv/pallas_call | solution.py:249
  46.8 19.6 %all_to_all.11.got_ref = bf16[16,64,128]{2,1,0:T(8,128)(2,1)S(1)} all-to-all(bf16[16,64,128]{2,1,0:T(8,128)(2,1)S(1)} %conv.1), channel_id=1, replica_groups=mesh['gx'=16,'ch'=16] {'ch'}, dimensions={0} | all-to-all | bytes 524288 | tf_op jit(solution)/shard_map/all_to_all | solution.py:261
  66.5 0.9 %unpack.1 = (bf16[8,16,4,128]{3,2,1,0:T(4,128)(2,1)}, bf16[8,16,4,128]{3,2,1,0:T(4,128)(2,1)}) custom-call(bf16[16,64,128]{2,1,0:T(8,128)(2,1)S(1)} %all_to_all.11.got_ref), custom_call_target="tpu_custom_call" | custom-call | tf_op jit(solution)/shard_map/unpack/pallas_call | solution.py:262
  (3 shorter events, 0.1 us)
Async XLA Ops:
  31.9 6.1 %collective-permute-start.3 = (bf16[16,56,128]{2,1,0:T(8,128)(2,1)S(1)}, bf16[16,56,128]{2,1,0:T(8,128)(2,1)S(1)}, u32[]{:S(2)}, u32[]{:S(2)}) collective-permute-start(bf16[16,56,128]{2,1,0:T(8,128)(2,1)S(1)} %slice.19.own_ref), channel_id=1, source_target_pairs={{0,32},{16,48},{32,0},{48,16},{64,96},{80,112},{96,64},{112,80},{1... | collective-permute-start | bytes 688136 | tf_op jit(solution)/shard_map/ppermute | solution.py:228
  32.5 7.4 %collective-permute-start.2 = (bf16[16,56,128]{2,1,0:T(8,128)(2,1)S(1)}, bf16[16,56,128]{2,1,0:T(8,128)(2,1)S(1)}, u32[]{:S(2)}, u32[]{:S(2)}) collective-permute-start(bf16[16,56,128]{2,1,0:T(8,128)(2,1)S(1)} %slice.19.own_ref), channel_id=1, source_target_pairs={{0,16},{16,0},{32,48},{48,32},{64,80},{80,64},{96,112},{112,96},{1... | collective-permute-start | bytes 688136 | tf_op jit(solution)/shard_map/ppermute | solution.py:229
  38.0 1.9 %collective-permute-start.4 = (bf16[16,56,128]{2,1,0:T(8,128)(2,1)S(1)}, bf16[16,56,128]{2,1,0:T(8,128)(2,1)S(1)}, u32[]{:S(2)}, u32[]{:S(2)}) collective-permute-start(bf16[16,56,128]{2,1,0:T(8,128)(2,1)S(1)} %collective-permute-done.3.x_ref), channel_id=1, source_target_pairs={{0,16},{16,0},{32,48},{48,32},{64,80},{80,64},{96,112},{112,96},{1... | collective-permute-start | bytes 688136 | tf_op jit(solution)/shard_map/ppermute | solution.py:230
  38.0 4.8 %collective-permute-start = (bf16[16,40,128]{2,1,0:T(8,128)(2,1)S(1)}, bf16[16,40,128]{2,1,0:T(8,128)(2,1)S(1)}, u32[]{:S(2)}, u32[]{:S(2)}) collective-permute-start(bf16[16,40,128]{2,1,0:T(8,128)(2,1)S(1)} %get-tuple-element.7), channel_id=1, source_target_pairs={{0,2},{2,4},{4,6},{6,8},{8,10},{10,12},{12,14},{14,30},{30,28},{28... | collective-permute-start | bytes 491528 | tf_op jit(solution)/shard_map/ppermute | solution.py:237
  38.1 6.6 %collective-permute-start.1 = (bf16[16,40,128]{2,1,0:T(8,128)(2,1)S(1)}, bf16[16,40,128]{2,1,0:T(8,128)(2,1)S(1)}, u32[]{:S(2)}, u32[]{:S(2)}) collective-permute-start(bf16[16,40,128]{2,1,0:T(8,128)(2,1)S(1)} %get-tuple-element.6), channel_id=1, source_target_pairs={{2,0},{4,2},{6,4},{8,6},{10,8},{12,10},{14,12},{30,14},{28,30},{26... | collective-permute-start | bytes 491528 | tf_op jit(solution)/shard_map/ppermute | solution.py:238
where the time goes:
time: 67.5 us; the launch traced here: 67.3 us
  blocking collectives  49.4 us (73%)
  waiting for transfers between devices  9.85 us (15%)
  Pallas kernels  4.83 us (7%)
  starting transfers between devices  2.46 us (4%)
  between operations  0.68 us (1%)
    all_to_all x1, blocking collectives, local(): got = lax.all_to_all(send, 'ch', 0, 0, tiled=True)  29.8 us
    all_to_all x1, blocking collectives, local(): back = lax.all_to_all(result, 'ch', 0, 0, tiled=True)  19.6 us
    ppermute x1, waiting for transfers between devices, local(): x_filters = lax.ppermute(own_filters, 'gx', across_x)  5.48 us
    ppermute x1, waiting for transfers between devices, local(): low = lax.ppermute(got[:, block:span], ('gx', 'ch'), ring)  2.5 us
    pallas_call x1, Pallas kernels, local(): pl.pallas_call(functools.partial(conv_kernel, depth=depth), out_shape=jax...  2.11 us
    ppermute x1, waiting for transfers between devices, local(): lax.ppermute(got[:, :block + rows], ('gx', 'ch'), [(to, at) for at, to in...  1.87 us
    ppermute x1, starting transfers between devices, local(): lax.ppermute(got[:, :block + rows], ('gx', 'ch'), [(to, at) for at, to in...  1.73 us
    pallas_call x1, Pallas kernels, local(): pl.pallas_call(pack_kernel, out_shape=jax.ShapeDtypeStruct((count, span +...  1.4 us
  transfers between devices with their start and end apart: 5, of which 3 were waited for; matrix products, arithmetic and copies ran while one was open for 0% of the time, Pallas kernels for 1%

commit v1 on v0

--- a/solution.py
+++ b/solution.py
@@ -23,9 +23,20 @@
     return level + core * (count // 2 - 1 - 2 * level)
 
 
-def quarter(taps, index):
-    size = (taps + 3) // 4
+def share(taps, index):
+    size = (taps + 7) // 8
     return (min(index * size, taps - size) if isinstance(index, int) else jnp.minimum(index * size, taps - size)), size
+
+
+def share_of(slab):
+    return lax.rem(slab, 4) + 4 * (slab // 8)
+
+
+def flip(index, bits):
+    for bit in (1, 2, 4):
+        if bits & bit:
+            index = index + bit - 2 * bit * lax.rem(index // bit, 2)
+    return index
 
 
 def both(first, second):
@@ -74,20 +85,22 @@
         for half in range(2):
             send_ref[2 * level + half, block : block + rows, :] = edges[half].astype(BF16)
     copies[2].wait()
-    first, shared = quarter(taps, lax.rem(lax.axis_index("gx"), 4))
+    first, shared = share(taps, share_of(lax.axis_index("gx")))
     filters = weight_ref[pl.ds(first, shared)].reshape(shared * rows, fan)
     for chip in range(count):
         send_ref[chip, 2 * block + rows :, :] = filters
 
 
-def prepare_kernel(own_ref, core_ref, x_ref, diagonal_ref, forward_ref, backward_ref, filters_ref, *, taps):
+def prepare_kernel(own_ref, core_ref, near_ref, across_ref, forward_ref, backward_ref, filters_ref, *, taps):
     count, _, channels = own_ref.shape
     rows = channels // count
-    mine = lax.rem(lax.axis_index("gx"), 4)
-    core, x = lax.rem(mine, 2), mine // 2
-    for at, ref in ((2 * x + core, own_ref), (2 * x + 1 - core, core_ref),
-                    (2 - 2 * x + core, x_ref), (3 - 2 * x - core, diagonal_ref)):
-        filters_ref[at] = ref[...]
+    mine = share_of(lax.axis_index("gx"))
+    filters_ref[mine] = own_ref[...]
+    filters_ref[flip(mine, 1)] = core_ref[...]
+    for at, step in enumerate((2, 4, 6)):
+        there = flip(mine, step)
+        filters_ref[there] = near_ref[at * count : (at + 1) * count]
+        filters_ref[flip(there, 1)] = across_ref[at * count : (at + 1) * count]
 
     def spot(index):
         return slice(index * channels, (index + 1) * channels)
@@ -96,8 +109,8 @@
         for b in range(3):
             for c in range(3):
                 tap = 9 * a + 3 * b + c
-                part = tap // quarter(taps, 0)[1]
-                at = tap - quarter(taps, part)[0]
+                part = tap // share(taps, 0)[1]
+                at = tap - share(taps, part)[0]
                 matrix = filters_ref[part, :, at * rows : (at + 1) * rows, :].reshape(channels, channels)
                 forward_ref[spot(b), spot(3 * c + a)] = matrix
                 backward_ref[spot(b), spot(3 * c + a)] = matrix.T
@@ -205,7 +218,7 @@
     taps, channels, _ = conv_weight.shape
     block = rows * depth
     span = 2 * block + rows
-    shared = quarter(taps, 0)[1]
+    shared = share(taps, 0)[1]
     pairs = count // 2
     send = pl.pallas_call(
         pack_kernel,
@@ -224,10 +237,13 @@
     )(*(pltpu.with_memory_space_constraint(x, pltpu.HBM) for x in (activations, out_grad, jnp.swapaxes(conv_weight, 1, 2))))
     got = lax.all_to_all(send, "ch", 0, 0, tiled=True)
     own, own_filters = got[:, :span], got[:, span:]
-    across_core, across_x = ([(slab, slab ^ step) for slab in range(slabs)] for step in (1, 2))
-    x_filters = lax.ppermute(own_filters, "gx", across_x)
+    across_core, *pairs_near = ([(slab, slab ^ step) for slab in range(slabs)] for step in (1, 2, 8, 10))
+    near_filters = []
+    for route in pairs_near:
+        near_filters.append(lax.ppermute(own_filters, "gx", route))
+    near_filters = jnp.concatenate(near_filters)
     core_filters = lax.ppermute(own_filters, "gx", across_core)
-    diagonal_filters = lax.ppermute(x_filters, "gx", across_core)
+    diagonal_filters = lax.ppermute(near_filters, "gx", across_core)
     ring = []
     for side in range(2):
         order = [
@@ -241,11 +257,11 @@
         out_shape=[jax.ShapeDtypeStruct((3 * channels, 9 * channels), BF16)] * 2,
         in_specs=[VMEM, VMEM, VMEM, VMEM],
         out_specs=[VMEM, VMEM],
-        scratch_shapes=[pltpu.VMEM((4, count, shared * rows, channels), BF16)],
+        scratch_shapes=[pltpu.VMEM((8, count, shared * rows, channels), BF16)],
         cost_estimate=pl.CostEstimate(flops=0, bytes_accessed=4 * 2**20, transcendentals=0),
         compiler_params=PARAMS,
         name="prepare",
-    )(own_filters, core_filters, x_filters, diagonal_filters)
+    )(own_filters, core_filters, near_filters, diagonal_filters)
     result = pl.pallas_call(
         functools.partial(conv_kernel, depth=depth),
         out_shape=jax.ShapeDtypeStruct((count, 2 * block, height), BF16),

time: 67.5 us -> 67.2 us (level)
  starting transfers between devices: 2.46 us -> 6.36 us
  waiting for transfers between devices: 9.85 us -> 7.22 us
  blocking collectives: 49.4 us -> 47.4 us
    ppermute x2 -> x4, starting transfers between devices: 0.62 us -> 3.67 us  [the longest x3 3.58 us: local(): near_filters.append(lax.ppermute(own_filters, 'gx', route))]
    all_to_all x1, blocking collectives: 29.8 us -> 27.5 us  [local(): got = lax.all_to_all(send, 'ch', 0, 0, tiled=True)]
    ppermute x2 -> x4, waiting for transfers between devices: 5.49 us -> 3.7 us  [the longest x3 3.69 us: local(): near_filters.append(lax.ppermute(own_filters, 'gx', route))]
    ppermute x1, waiting for transfers between devices: 2.5 us -> 1.01 us  [local(): low = lax.ppermute(got[:, block:span], ('gx', 'ch'), ring)]
    ppermute x1, waiting for transfers between devices: 0.01 us -> 0.96 us  [local(): core_filters = lax.ppermute(own_filters, 'gx', across_core)]
  transfers between devices with their start and end apart: 5 -> 7, of which waited for: 3 -> 5; matrix products, arithmetic and copies ran while one was open for 0% -> 0% of each run, Pallas kernels for 1% -> 1%
where the time goes in v1:
time: 67.2 us; the launch traced here: 66.6 us
  blocking collectives  47.4 us (71%)
  waiting for transfers between devices  7.22 us (11%)
  starting transfers between devices  6.36 us (9%)
  Pallas kernels  4.8 us (7%)
  between operations  0.7 us (1%)
    all_to_all x1, blocking collectives, local(): got = lax.all_to_all(send, 'ch', 0, 0, tiled=True)  27.5 us
    all_to_all x1, blocking collectives, local(): back = lax.all_to_all(result, 'ch', 0, 0, tiled=True)  19.9 us
    ppermute x3, waiting for transfers between devices, local(): near_filters.append(lax.ppermute(own_filters, 'gx', route))  3.69 us
    ppermute x3, starting transfers between devices, local(): near_filters.append(lax.ppermute(own_filters, 'gx', route))  3.58 us
    pallas_call x1, Pallas kernels, local(): pl.pallas_call(functools.partial(conv_kernel, depth=depth), out_shape=jax...  2.11 us
    ppermute x1, waiting for transfers between devices, local(): lax.ppermute(got[:, :block + rows], ('gx', 'ch'), [(to, at) for at, to in...  1.55 us
    ppermute x1, starting transfers between devices, local(): lax.ppermute(got[:, :block + rows], ('gx', 'ch'), [(to, at) for at, to in...  1.51 us
    pallas_call x1, Pallas kernels, local(): pl.pallas_call(pack_kernel, out_shape=jax.ShapeDtypeStruct((count, span +...  1.37 us
  transfers between devices with their start and end apart: 7, of which 5 were waited for; matrix products, arithmetic and copies ran while one was open for 0% of the time, Pallas kernels for 1%

profile of v1, /device:TPU:2, one launch (start us, length us, event | category | flops | bytes accessed | tf_op | source)
XLA Modules:
  0.0 66.6 jit_solution(3849212755642772476)
XLA Ops:
  0.6 1.4 %pack.1 = bf16[16,104,128]{2,1,0:T(8,128)(2,1)S(1)} custom-call(bf16[8,16,4,128]{3,2,1,0:T(4,128)(2,1)} %act_hbm.1, bf16[8,16,4,128]{3,2,1,0:T(4,128)(2,1)} %grad_hbm.1, bf16[27,8,128]{2,1,0:T(8,128)(2,1)} %bitcast.1), custom_call_target="tpu_custom_call" | custom-call | tf_op jit(solution)/shard_map/pack/pallas_call | solution.py:223
  2.0 27.5 %all_to_all.10 = bf16[16,104,128]{2,1,0:T(8,128)(2,1)S(1)} all-to-all(bf16[16,104,128]{2,1,0:T(8,128)(2,1)S(1)} %pack.1), channel_id=1, replica_groups=mesh['gx'=16,'ch'=16] {'ch'}, dimensions={0} | all-to-all | bytes 851968 | tf_op jit(solution)/shard_map/all_to_all | solution.py:238
  29.6 0.6 collective-permute-start.3
  30.2 0.7 %collective-permute-start.4 = (bf16[16,32,128]{2,1,0:T(8,128)(2,1)S(1)}, bf16[16,32,128]{2,1,0:T(8,128)(2,1)S(1)}, u32[]{:S(2)}, u32[]{:S(2)}) collective-permute-start(bf16[16,32,128]{2,1,0:T(8,128)(2,1)S(1)} %slice.19.own_ref), channel_id=1, source_target_pairs={{0,128},{16,144},{32,160},{48,176},{64,192},{80,208},{96,224},{112... | collective-permute-start | bytes 393224 | tf_op jit(solution)/shard_map/ppermute | solution.py:243
  30.9 2.3 %collective-permute-start.5 = (bf16[16,32,128]{2,1,0:T(8,128)(2,1)S(1)}, bf16[16,32,128]{2,1,0:T(8,128)(2,1)S(1)}, u32[]{:S(2)}, u32[]{:S(2)}) collective-permute-start(bf16[16,32,128]{2,1,0:T(8,128)(2,1)S(1)} %slice.19.own_ref), channel_id=1, source_target_pairs={{0,160},{16,176},{32,128},{48,144},{64,224},{80,240},{96,192},{112... | collective-permute-start | bytes 393224 | tf_op jit(solution)/shard_map/ppermute | solution.py:243
  33.1 2.0 %collective-permute-done.3 = bf16[16,32,128]{2,1,0:T(8,128)(2,1)S(1)} collective-permute-done((bf16[16,32,128]{2,1,0:T(8,128)(2,1)S(1)}, bf16[16,32,128]{2,1,0:T(8,128)(2,1)S(1)}, u32[]{:S(2)}, u32[]{:S(2)}) %collective-permute-start.3) | collective-permute-done | bytes 131104 | tf_op jit(solution)/shard_map/ppermute | solution.py:243
  35.1 1.7 %collective-permute-done.4 = bf16[16,32,128]{2,1,0:T(8,128)(2,1)S(1)} collective-permute-done((bf16[16,32,128]{2,1,0:T(8,128)(2,1)S(1)}, bf16[16,32,128]{2,1,0:T(8,128)(2,1)S(1)}, u32[]{:S(2)}, u32[]{:S(2)}) %collective-permute-start.4) | collective-permute-done | bytes 131104 | tf_op jit(solution)/shard_map/ppermute | solution.py:243
  36.9 0.0 collective-permute-done.5
  36.9 0.1 collective-permute-start.6
  37.0 0.7 %collective-permute-start = (bf16[16,40,128]{2,1,0:T(8,128)(2,1)S(1)}, bf16[16,40,128]{2,1,0:T(8,128)(2,1)S(1)}, u32[]{:S(2)}, u32[]{:S(2)}) collective-permute-start(bf16[16,40,128]{2,1,0:T(8,128)(2,1)S(1)} %get-tuple-element.7), channel_id=1, source_target_pairs={{0,2},{2,4},{4,6},{6,8},{8,10},{10,12},{12,14},{14,30},{30,28},{28... | collective-permute-start | bytes 491528 | tf_op jit(solution)/shard_map/ppermute | solution.py:253
  37.8 1.5 %collective-permute-start.1 = (bf16[16,40,128]{2,1,0:T(8,128)(2,1)S(1)}, bf16[16,40,128]{2,1,0:T(8,128)(2,1)S(1)}, u32[]{:S(2)}, u32[]{:S(2)}) collective-permute-start(bf16[16,40,128]{2,1,0:T(8,128)(2,1)S(1)} %get-tuple-element.6), channel_id=1, source_target_pairs={{2,0},{4,2},{6,4},{8,6},{10,8},{12,10},{14,12},{30,14},{28,30},{26... | collective-permute-start | bytes 491528 | tf_op jit(solution)/shard_map/ppermute | solution.py:254
  39.3 0.5 collective-permute-start.2
  39.8 1.0 %collective-permute-done.2.core_ref = bf16[16,32,128]{2,1,0:T(8,128)(2,1)S(1)} collective-permute-done((bf16[16,32,128]{2,1,0:T(8,128)(2,1)S(1)}, bf16[16,32,128]{2,1,0:T(8,128)(2,1)S(1)}, u32[]{:S(2)}, u32[]{:S(2)}) %collective-permute-start.2) | collective-permute-done | bytes 131104 | tf_op jit(solution)/shard_map/ppermute | solution.py:245
  40.7 0.0 collective-permute-done.6.across_ref
  40.7 0.4 prepare.1
  41.2 1.0 %collective-permute-done.low_ref = bf16[16,40,128]{2,1,0:T(8,128)(2,1)S(1)} collective-permute-done((bf16[16,40,128]{2,1,0:T(8,128)(2,1)S(1)}, bf16[16,40,128]{2,1,0:T(8,128)(2,1)S(1)}, u32[]{:S(2)}, u32[]{:S(2)}) %collective-permute-start) | collective-permute-done | bytes 163872 | tf_op jit(solution)/shard_map/ppermute | solution.py:253
  42.2 1.6 %collective-permute-done.1.high_ref = bf16[16,40,128]{2,1,0:T(8,128)(2,1)S(1)} collective-permute-done((bf16[16,40,128]{2,1,0:T(8,128)(2,1)S(1)}, bf16[16,40,128]{2,1,0:T(8,128)(2,1)S(1)}, u32[]{:S(2)}, u32[]{:S(2)}) %collective-permute-start.1) | collective-permute-done | bytes 163872 | tf_op jit(solution)/shard_map/ppermute | solution.py:254
  43.7 2.1 %conv.1 = bf16[16,64,128]{2,1,0:T(8,128)(2,1)S(1)} custom-call(bf16[16,72,128]{2,1,0:T(8,128)(2,1)S(1)} %slice.16.own_ref, bf16[16,40,128]{2,1,0:T(8,128)(2,1)S(1)} %collective-permute-done.low_ref, bf16[16,40,128]{2,1,0:T(8,128)(2,1)S(1)} %collective-permute-done.1.high_ref, bf16[384,1152]{1,0:T(8,128)(2,1)S(1)} %get-tuple-element.4.forward_ref, ...), custom_call_target="tpu_custom_call" | custom-call | tf_op jit(solution)/shard_map/conv/pallas_call | solution.py:265
  45.8 19.9 %all_to_all.11.got_ref = bf16[16,64,128]{2,1,0:T(8,128)(2,1)S(1)} all-to-all(bf16[16,64,128]{2,1,0:T(8,128)(2,1)S(1)} %conv.1), channel_id=1, replica_groups=mesh['gx'=16,'ch'=16] {'ch'}, dimensions={0} | all-to-all | bytes 524288 | tf_op jit(solution)/shard_map/all_to_all | solution.py:277
  65.7 0.9 %unpack.1 = (bf16[8,16,4,128]{3,2,1,0:T(4,128)(2,1)}, bf16[8,16,4,128]{3,2,1,0:T(4,128)(2,1)}) custom-call(bf16[16,64,128]{2,1,0:T(8,128)(2,1)S(1)} %all_to_all.11.got_ref), custom_call_target="tpu_custom_call" | custom-call | tf_op jit(solution)/shard_map/unpack/pallas_call | solution.py:278
  (6 shorter events, 0.1 us)
Async XLA Ops:
  29.6 5.6 %collective-permute-start.3 = (bf16[16,32,128]{2,1,0:T(8,128)(2,1)S(1)}, bf16[16,32,128]{2,1,0:T(8,128)(2,1)S(1)}, u32[]{:S(2)}, u32[]{:S(2)}) collective-permute-start(bf16[16,32,128]{2,1,0:T(8,128)(2,1)S(1)} %slice.19.own_ref), channel_id=1, source_target_pairs={{0,32},{16,48},{32,0},{48,16},{64,96},{80,112},{96,64},{112,80},{1... | collective-permute-start | bytes 393224 | tf_op jit(solution)/shard_map/ppermute | solution.py:243
  30.2 6.7 %collective-permute-start.4 = (bf16[16,32,128]{2,1,0:T(8,128)(2,1)S(1)}, bf16[16,32,128]{2,1,0:T(8,128)(2,1)S(1)}, u32[]{:S(2)}, u32[]{:S(2)}) collective-permute-start(bf16[16,32,128]{2,1,0:T(8,128)(2,1)S(1)} %slice.19.own_ref), channel_id=1, source_target_pairs={{0,128},{16,144},{32,160},{48,176},{64,192},{80,208},{96,224},{112... | collective-permute-start | bytes 393224 | tf_op jit(solution)/shard_map/ppermute | solution.py:243
  30.9 6.0 %collective-permute-start.5 = (bf16[16,32,128]{2,1,0:T(8,128)(2,1)S(1)}, bf16[16,32,128]{2,1,0:T(8,128)(2,1)S(1)}, u32[]{:S(2)}, u32[]{:S(2)}) collective-permute-start(bf16[16,32,128]{2,1,0:T(8,128)(2,1)S(1)} %slice.19.own_ref), channel_id=1, source_target_pairs={{0,160},{16,176},{32,128},{48,144},{64,224},{80,240},{96,192},{112... | collective-permute-start | bytes 393224 | tf_op jit(solution)/shard_map/ppermute | solution.py:243
  36.9 3.8 %collective-permute-start.6 = (bf16[48,32,128]{2,1,0:T(8,128)(2,1)S(1)}, bf16[48,32,128]{2,1,0:T(8,128)(2,1)S(1)}, u32[]{:S(2)}, u32[]{:S(2)}) collective-permute-start(bf16[48,32,128]{2,1,0:T(8,128)(2,1)S(1)} %constant_dynamic-update-slice_fusion.near_ref), channel_id=1, source_target_pairs={{0,16},{16,0},{32,48},{48,32},{64,80},{80,64},{96,112},{112,96},{1... | collective-permute-start | bytes 1179656 | tf_op jit(solution)/shard_map/ppermute | solution.py:246
  37.0 5.1 %collective-permute-start = (bf16[16,40,128]{2,1,0:T(8,128)(2,1)S(1)}, bf16[16,40,128]{2,1,0:T(8,128)(2,1)S(1)}, u32[]{:S(2)}, u32[]{:S(2)}) collective-permute-start(bf16[16,40,128]{2,1,0:T(8,128)(2,1)S(1)} %get-tuple-element.7), channel_id=1, source_target_pairs={{0,2},{2,4},{4,6},{6,8},{8,10},{10,12},{12,14},{14,30},{30,28},{28... | collective-permute-start | bytes 491528 | tf_op jit(solution)/shard_map/ppermute | solution.py:253
  37.8 6.0 %collective-permute-start.1 = (bf16[16,40,128]{2,1,0:T(8,128)(2,1)S(1)}, bf16[16,40,128]{2,1,0:T(8,128)(2,1)S(1)}, u32[]{:S(2)}, u32[]{:S(2)}) collective-permute-start(bf16[16,40,128]{2,1,0:T(8,128)(2,1)S(1)} %get-tuple-element.6), channel_id=1, source_target_pairs={{2,0},{4,2},{6,4},{8,6},{10,8},{12,10},{14,12},{30,14},{28,30},{26... | collective-permute-start | bytes 491528 | tf_op jit(solution)/shard_map/ppermute | solution.py:254
  39.3 1.5 %collective-permute-start.2 = (bf16[16,32,128]{2,1,0:T(8,128)(2,1)S(1)}, bf16[16,32,128]{2,1,0:T(8,128)(2,1)S(1)}, u32[]{:S(2)}, u32[]{:S(2)}) collective-permute-start(bf16[16,32,128]{2,1,0:T(8,128)(2,1)S(1)} %slice.19.own_ref), channel_id=1, source_target_pairs={{0,16},{16,0},{32,48},{48,32},{64,80},{80,64},{96,112},{112,96},{1... | collective-permute-start | bytes 393224 | tf_op jit(solution)/shard_map/ppermute | solution.py:245

commit v2 on v0

--- a/solution.py
+++ b/solution.py
@@ -23,9 +23,12 @@
     return level + core * (count // 2 - 1 - 2 * level)
 
 
-def quarter(taps, index):
-    size = (taps + 3) // 4
-    return (min(index * size, taps - size) if isinstance(index, int) else jnp.minimum(index * size, taps - size)), size
+GROUPS = ((0, 4), (15, 3))
+
+
+def place_of(slab):
+    core, x, y = lax.rem(slab, 2), lax.rem(slab // 2, 2), slab // 8
+    return core, (x, y)
 
 
 def both(first, second):
@@ -46,7 +49,7 @@
         copy.start()
     core = lax.rem(lax.axis_index("gx"), 2)
     count, (rows, _, depth, height) = send_ref.shape[0], act_ref.shape
-    taps, _, fan = weight_ref.shape
+    _, _, fan = weight_ref.shape
     block = rows * depth
     side = height // 2
     copies[0].wait()
@@ -74,20 +77,26 @@
         for half in range(2):
             send_ref[2 * level + half, block : block + rows, :] = edges[half].astype(BF16)
     copies[2].wait()
-    first, shared = quarter(taps, lax.rem(lax.axis_index("gx"), 4))
-    filters = weight_ref[pl.ds(first, shared)].reshape(shared * rows, fan)
-    for chip in range(count):
-        send_ref[chip, 2 * block + rows :, :] = filters
-
-
-def prepare_kernel(own_ref, core_ref, x_ref, diagonal_ref, forward_ref, backward_ref, filters_ref, *, taps):
+    start = 2 * block + rows
+    for (first, size), place in zip(GROUPS, place_of(lax.axis_index("gx"))[1]):
+        filters = weight_ref[pl.ds(first + size * (core + 2 * place), size)].reshape(size * rows, fan)
+        for chip in range(count):
+            send_ref[chip, start : start + size * rows, :] = filters
+        start += size * rows
+
+
+def prepare_kernel(own_ref, core_ref, x_ref, y_ref, diagonal_ref, forward_ref, backward_ref, *filters_refs):
     count, _, channels = own_ref.shape
     rows = channels // count
-    mine = lax.rem(lax.axis_index("gx"), 4)
-    core, x = lax.rem(mine, 2), mine // 2
-    for at, ref in ((2 * x + core, own_ref), (2 * x + 1 - core, core_ref),
-                    (2 - 2 * x + core, x_ref), (3 - 2 * x - core, diagonal_ref)):
-        filters_ref[at] = ref[...]
+    core, places = place_of(lax.axis_index("gx"))
+    start = 0
+    for (_, size), place, filters_ref, near_ref in zip(GROUPS, places, filters_refs, (x_ref, y_ref)):
+        span = slice(start, start + size * rows)
+        filters_ref[2 * place + core] = own_ref[:, span, :]
+        filters_ref[2 * place + 1 - core] = core_ref[:, span, :]
+        filters_ref[2 - 2 * place + core] = near_ref[...]
+        filters_ref[3 - 2 * place - core] = diagonal_ref[:, span, :]
+        start += size * rows
 
     def spot(index):
         return slice(index * channels, (index + 1) * channels)
@@ -96,20 +105,22 @@
         for b in range(3):
             for c in range(3):
                 tap = 9 * a + 3 * b + c
-                part = tap // quarter(taps, 0)[1]
-                at = tap - quarter(taps, part)[0]
-                matrix = filters_ref[part, :, at * rows : (at + 1) * rows, :].reshape(channels, channels)
+                group = 0 if tap < GROUPS[1][0] else 1
+                part, at = divmod(tap - GROUPS[group][0], GROUPS[group][1])
+                matrix = filters_refs[group][part, :, at * rows : (at + 1) * rows, :].reshape(channels, channels)
                 forward_ref[spot(b), spot(3 * c + a)] = matrix
                 backward_ref[spot(b), spot(3 * c + a)] = matrix.T
 
 
-def conv_kernel(own_ref, low_ref, high_ref, forward_ref, backward_ref, send_ref, cells_ref, wide_ref, *, depth):
+def conv_kernel(own_ref, low_ref, high_ref, forward_ref, backward_ref, send_ref,
+                forward_cells_ref, backward_cells_ref, wide_ref, *, depth):
     count, span, height = own_ref.shape
     rows = span // (2 * depth + 1)
     block = rows * depth
     channels = count * rows
     side = height // 2
     right = lax.rem(lax.axis_index("ch"), 2)
+    cells_refs = (forward_cells_ref, backward_cells_ref)
 
     def spot(index):
         return slice(index * channels, (index + 1) * channels)
@@ -141,7 +152,7 @@
             direction = 1 - 2 * tensor
             outside = 0 if direction * (c - 1) < 0 else depth - 1
             if c != 1:
-                cells_ref[tensor, 3 * c * channels : 3 * (c + 1) * channels, outside * height : (outside + 1) * height] = (
+                cells_refs[tensor][3 * c * channels : 3 * (c + 1) * channels, outside * height : (outside + 1) * height] = (
                     jnp.zeros((3 * channels, height), BF16)
                 )
             for a in range(3):
@@ -150,7 +161,7 @@
                 source = within + direction * (c - 1)
                 inside = (within < depth) & (source >= 0) & (source < depth)
                 moved = pltpu.roll(edge, -shift % height, 1)
-                cells_ref[tensor, spot(3 * c + a), depth * height :] = jnp.where(inside, moved, 0.0).astype(BF16)
+                cells_refs[tensor][spot(3 * c + a), depth * height :] = jnp.where(inside, moved, 0.0).astype(BF16)
     for z in range(depth):
         pieces = [wide_ref[at, pl.ds(z, channels, stride=depth), :] for at in range(4)]
         for step in range(3):
@@ -161,14 +172,15 @@
                 for c in range(3):
                     target = z - direction * (c - 1)
                     if 0 <= target < depth:
-                        cells_ref[tensor, spot(3 * c + a), target * height : (target + 1) * height] = values
+                        cells_refs[tensor][spot(3 * c + a), target * height : (target + 1) * height] = values
 
     for tensor in range(2):
         direction = 1 - 2 * tensor
-        filters = (forward_ref, backward_ref)[tensor][...]
-        sums = jnp.dot(filters, cells_ref[tensor], preferred_element_type=F32)
-        beyond = sums[:, depth * height :]
-        beyond = jnp.where(right == 1, beyond[spot(1 - direction)], beyond[spot(1 + direction)])
+        filters_ref = (forward_ref, backward_ref)[tensor]
+        sums = jnp.dot(filters_ref[...], cells_refs[tensor][:, : depth * height], preferred_element_type=F32)
+        b = pl.multiple_of((1 + direction - 2 * direction * right) * channels, channels)
+        beyond = jnp.dot(filters_ref[pl.ds(b, channels), :], cells_refs[tensor][:, depth * height :],
+                         preferred_element_type=F32)
         border = jnp.where(right == 1, 0, side - 1)
         for z in range(depth):
             columns = slice(z * height, (z + 1) * height)
@@ -205,11 +217,12 @@
     taps, channels, _ = conv_weight.shape
     block = rows * depth
     span = 2 * block + rows
-    shared = quarter(taps, 0)[1]
+    sizes = [size * rows for _, size in GROUPS]
+    shared = sum(sizes)
     pairs = count // 2
     send = pl.pallas_call(
         pack_kernel,
-        out_shape=jax.ShapeDtypeStruct((count, span + shared * rows, height), BF16),
+        out_shape=jax.ShapeDtypeStruct((count, span + shared, height), BF16),
         in_specs=[HBM, HBM, HBM],
         out_specs=VMEM,
         scratch_shapes=[
@@ -224,10 +237,11 @@
     )(*(pltpu.with_memory_space_constraint(x, pltpu.HBM) for x in (activations, out_grad, jnp.swapaxes(conv_weight, 1, 2))))
     got = lax.all_to_all(send, "ch", 0, 0, tiled=True)
     own, own_filters = got[:, :span], got[:, span:]
-    across_core, across_x = ([(slab, slab ^ step) for slab in range(slabs)] for step in (1, 2))
-    x_filters = lax.ppermute(own_filters, "gx", across_x)
+    across_core, across_x, across_y = ([(slab, slab ^ step) for slab in range(slabs)] for step in (1, 2, 8))
+    x_filters = lax.ppermute(got[:, span : span + sizes[0]], "gx", across_x)
+    y_filters = lax.ppermute(got[:, span + sizes[0] :], "gx", across_y)
     core_filters = lax.ppermute(own_filters, "gx", across_core)
-    diagonal_filters = lax.ppermute(x_filters, "gx", across_core)
+    diagonal_filters = lax.ppermute(jnp.concatenate([x_filters, y_filters], axis=1), "gx", across_core)
     ring = []
     for side in range(2):
         order = [
@@ -237,22 +251,23 @@
     low = lax.ppermute(got[:, block:span], ("gx", "ch"), ring)
     high = lax.ppermute(got[:, : block + rows], ("gx", "ch"), [(to, at) for at, to in ring])
     forward, backward = pl.pallas_call(
-        functools.partial(prepare_kernel, taps=taps),
+        prepare_kernel,
         out_shape=[jax.ShapeDtypeStruct((3 * channels, 9 * channels), BF16)] * 2,
-        in_specs=[VMEM, VMEM, VMEM, VMEM],
+        in_specs=[VMEM] * 5,
         out_specs=[VMEM, VMEM],
-        scratch_shapes=[pltpu.VMEM((4, count, shared * rows, channels), BF16)],
+        scratch_shapes=[pltpu.VMEM((4, count, size, channels), BF16) for size in sizes],
         cost_estimate=pl.CostEstimate(flops=0, bytes_accessed=4 * 2**20, transcendentals=0),
         compiler_params=PARAMS,
         name="prepare",
-    )(own_filters, core_filters, x_filters, diagonal_filters)
+    )(own_filters, core_filters, x_filters, y_filters, diagonal_filters)
     result = pl.pallas_call(
         functools.partial(conv_kernel, depth=depth),
         out_shape=jax.ShapeDtypeStruct((count, 2 * block, height), BF16),
         in_specs=[VMEM, VMEM, VMEM, VMEM, VMEM],
         out_specs=VMEM,
         scratch_shapes=[
-            pltpu.VMEM((2, 9 * channels, (depth + 1) * height), BF16),
+            pltpu.VMEM((9 * channels, (depth + 1) * height), BF16),
+            pltpu.VMEM((9 * channels, (depth + 1) * height), BF16),
             pltpu.VMEM((4, channels * depth, height), F32),
         ],
         compiler_params=PARAMS,

time: 67.5 us -> 65.8 us (0.975)
  waiting for transfers between devices: 9.85 us -> 8.1 us
  blocking collectives: 49.4 us -> 48.1 us
  starting transfers between devices: 2.46 us -> 3.4 us
    ppermute x2 -> x3, waiting for transfers between devices: 5.49 us -> 3.82 us  [the longest x1 3.82 us: local(): y_filters = lax.ppermute(got[:, span + sizes[0]:], 'gx', across_y)]
    all_to_all x1, blocking collectives: 19.6 us -> 18.3 us  [local(): back = lax.all_to_all(result, 'ch', 0, 0, tiled=True)]
    ppermute x2 -> x3, starting transfers between devices: 0.62 us -> 1.48 us  [the longest x1 0.76 us: local(): y_filters = lax.ppermute(got[:, span + sizes[0]:], 'gx', across_y)]
  transfers between devices with their start and end apart: 5 -> 6, of which waited for: 3 -> 3; matrix products, arithmetic and copies ran while one was open for 0% -> 0% of each run, Pallas kernels for 1% -> 1%
where the time goes in v2:
time: 65.8 us; the launch traced here: 65 us
  blocking collectives  48.1 us (73%)
  waiting for transfers between devices  8.1 us (12%)
  Pallas kernels  4.59 us (7%)
  starting transfers between devices  3.4 us (5%)
  between operations  0.72 us (1%)
    all_to_all x1, blocking collectives, local(): got = lax.all_to_all(send, 'ch', 0, 0, tiled=True)  29.8 us
    all_to_all x1, blocking collectives, local(): back = lax.all_to_all(result, 'ch', 0, 0, tiled=True)  18.3 us
    ppermute x1, waiting for transfers between devices, local(): y_filters = lax.ppermute(got[:, span + sizes[0]:], 'gx', across_y)  3.82 us
    ppermute x1, waiting for transfers between devices, local(): low = lax.ppermute(got[:, block:span], ('gx', 'ch'), ring)  2.43 us
    ppermute x1, waiting for transfers between devices, local(): lax.ppermute(got[:, :block + rows], ('gx', 'ch'), [(to, at) for at, to in...  1.85 us
    pallas_call x1, Pallas kernels, local(): pl.pallas_call(functools.partial(conv_kernel, depth=depth), out_shape=jax...  1.79 us
    ppermute x1, starting transfers between devices, local(): lax.ppermute(got[:, :block + rows], ('gx', 'ch'), [(to, at) for at, to in...  1.73 us
    pallas_call x1, Pallas kernels, local(): pl.pallas_call(pack_kernel, out_shape=jax.ShapeDtypeStruct((count, span +...  1.4 us
  transfers between devices with their start and end apart: 6, of which 3 were waited for; matrix products, arithmetic and copies ran while one was open for 0% of the time, Pallas kernels for 1%

profile of v2, /device:TPU:2, one launch (start us, length us, event | category | flops | bytes accessed | tf_op | source)
XLA Modules:
  0.0 65.0 jit_solution(13995790914143195590)
XLA Ops:
  0.6 1.4 %pack.1 = bf16[16,128,128]{2,1,0:T(8,128)(2,1)S(1)} custom-call(bf16[8,16,4,128]{3,2,1,0:T(4,128)(2,1)} %act_hbm.1, bf16[8,16,4,128]{3,2,1,0:T(4,128)(2,1)} %grad_hbm.1, bf16[27,8,128]{2,1,0:T(8,128)(2,1)} %bitcast.1), custom_call_target="tpu_custom_call" | custom-call | tf_op jit(solution)/shard_map/pack/pallas_call | solution.py:223
  2.0 29.8 %all_to_all.10 = bf16[16,128,128]{2,1,0:T(8,128)(2,1)S(1)} all-to-all(bf16[16,128,128]{2,1,0:T(8,128)(2,1)S(1)} %pack.1), channel_id=1, replica_groups=mesh['gx'=16,'ch'=16] {'ch'}, dimensions={0} | all-to-all | bytes 1048576 | tf_op jit(solution)/shard_map/all_to_all | solution.py:238
  31.9 0.6 collective-permute-start.3
  32.5 0.8 %collective-permute-start.4 = (bf16[16,24,128]{2,1,0:T(8,128)(2,1)S(1)}, bf16[16,24,128]{2,1,0:T(8,128)(2,1)S(1)}, u32[]{:S(2)}, u32[]{:S(2)}) collective-permute-start(bf16[16,24,128]{2,1,0:T(8,128)(2,1)S(1)} %slice.29), channel_id=1, source_target_pairs={{0,128},{16,144},{32,160},{48,176},{64,192},{80,208},{96,224},{112... | collective-permute-start | bytes 294920 | tf_op jit(solution)/shard_map/ppermute | solution.py:242
  33.3 0.1 collective-permute-start.2
  33.4 3.8 %collective-permute-done.4.y_ref = bf16[16,24,128]{2,1,0:T(8,128)(2,1)S(1)} collective-permute-done((bf16[16,24,128]{2,1,0:T(8,128)(2,1)S(1)}, bf16[16,24,128]{2,1,0:T(8,128)(2,1)S(1)}, u32[]{:S(2)}, u32[]{:S(2)}) %collective-permute-start.4) | collective-permute-done | bytes 98336 | tf_op jit(solution)/shard_map/ppermute | solution.py:242
  37.2 0.0 collective-permute-done.3.x_ref
  37.2 0.1 collective-permute-start.5
  37.4 0.1 collective-permute-start
  37.5 1.7 %collective-permute-start.1 = (bf16[16,40,128]{2,1,0:T(8,128)(2,1)S(1)}, bf16[16,40,128]{2,1,0:T(8,128)(2,1)S(1)}, u32[]{:S(2)}, u32[]{:S(2)}) collective-permute-start(bf16[16,40,128]{2,1,0:T(8,128)(2,1)S(1)} %get-tuple-element.6), channel_id=1, source_target_pairs={{2,0},{4,2},{6,4},{8,6},{10,8},{12,10},{14,12},{30,14},{28,30},{26... | collective-permute-start | bytes 491528 | tf_op jit(solution)/shard_map/ppermute | solution.py:252
  39.2 0.0 collective-permute-done.2.core_ref
  39.2 0.0 collective-permute-done.5.diagonal_ref
  39.3 0.5 prepare.1
  39.8 2.4 %collective-permute-done.low_ref = bf16[16,40,128]{2,1,0:T(8,128)(2,1)S(1)} collective-permute-done((bf16[16,40,128]{2,1,0:T(8,128)(2,1)S(1)}, bf16[16,40,128]{2,1,0:T(8,128)(2,1)S(1)}, u32[]{:S(2)}, u32[]{:S(2)}) %collective-permute-start) | collective-permute-done | bytes 163872 | tf_op jit(solution)/shard_map/ppermute | solution.py:251
  42.2 1.9 %collective-permute-done.1.high_ref = bf16[16,40,128]{2,1,0:T(8,128)(2,1)S(1)} collective-permute-done((bf16[16,40,128]{2,1,0:T(8,128)(2,1)S(1)}, bf16[16,40,128]{2,1,0:T(8,128)(2,1)S(1)}, u32[]{:S(2)}, u32[]{:S(2)}) %collective-permute-start.1) | collective-permute-done | bytes 163872 | tf_op jit(solution)/shard_map/ppermute | solution.py:252
  44.1 1.8 %conv.1 = bf16[16,64,128]{2,1,0:T(8,128)(2,1)S(1)} custom-call(bf16[16,72,128]{2,1,0:T(8,128)(2,1)S(1)} %slice.24.own_ref, bf16[16,40,128]{2,1,0:T(8,128)(2,1)S(1)} %collective-permute-done.low_ref, bf16[16,40,128]{2,1,0:T(8,128)(2,1)S(1)} %collective-permute-done.1.high_ref, bf16[384,1152]{1,0:T(8,128)(2,1)S(1)} %get-tuple-element.4.forward_ref, ...), custom_call_target="tpu_custom_call" | custom-call | tf_op jit(solution)/shard_map/conv/pallas_call | solution.py:263
  45.8 18.3 %all_to_all.11.got_ref = bf16[16,64,128]{2,1,0:T(8,128)(2,1)S(1)} all-to-all(bf16[16,64,128]{2,1,0:T(8,128)(2,1)S(1)} %conv.1), channel_id=1, replica_groups=mesh['gx'=16,'ch'=16] {'ch'}, dimensions={0} | all-to-all | bytes 524288 | tf_op jit(solution)/shard_map/all_to_all | solution.py:276
  64.1 0.9 %unpack.1 = (bf16[8,16,4,128]{3,2,1,0:T(4,128)(2,1)}, bf16[8,16,4,128]{3,2,1,0:T(4,128)(2,1)}) custom-call(bf16[16,64,128]{2,1,0:T(8,128)(2,1)S(1)} %all_to_all.11.got_ref), custom_call_target="tpu_custom_call" | custom-call | tf_op jit(solution)/shard_map/unpack/pallas_call | solution.py:277
  (6 shorter events, 0.1 us)
Async XLA Ops:
  31.9 5.3 %collective-permute-start.3 = (bf16[16,32,128]{2,1,0:T(8,128)(2,1)S(1)}, bf16[16,32,128]{2,1,0:T(8,128)(2,1)S(1)}, u32[]{:S(2)}, u32[]{:S(2)}) collective-permute-start(bf16[16,32,128]{2,1,0:T(8,128)(2,1)S(1)} %slice.28), channel_id=1, source_target_pairs={{0,32},{16,48},{32,0},{48,16},{64,96},{80,112},{96,64},{112,80},{1... | collective-permute-start | bytes 393224 | tf_op jit(solution)/shard_map/ppermute | solution.py:241
  32.5 4.7 %collective-permute-start.4 = (bf16[16,24,128]{2,1,0:T(8,128)(2,1)S(1)}, bf16[16,24,128]{2,1,0:T(8,128)(2,1)S(1)}, u32[]{:S(2)}, u32[]{:S(2)}) collective-permute-start(bf16[16,24,128]{2,1,0:T(8,128)(2,1)S(1)} %slice.29), channel_id=1, source_target_pairs={{0,128},{16,144},{32,160},{48,176},{64,192},{80,208},{96,224},{112... | collective-permute-start | bytes 294920 | tf_op jit(solution)/shard_map/ppermute | solution.py:242
  33.3 5.9 %collective-permute-start.2 = (bf16[16,56,128]{2,1,0:T(8,128)(2,1)S(1)}, bf16[16,56,128]{2,1,0:T(8,128)(2,1)S(1)}, u32[]{:S(2)}, u32[]{:S(2)}) collective-permute-start(bf16[16,56,128]{2,1,0:T(8,128)(2,1)S(1)} %slice.27.own_ref), channel_id=1, source_target_pairs={{0,16},{16,0},{32,48},{48,32},{64,80},{80,64},{96,112},{112,96},{1... | collective-permute-start | bytes 688136 | tf_op jit(solution)/shard_map/ppermute | solution.py:243
  37.2 2.0 %collective-permute-start.5 = (bf16[16,56,128]{2,1,0:T(8,128)(2,1)S(1)}, bf16[16,56,128]{2,1,0:T(8,128)(2,1)S(1)}, u32[]{:S(2)}, u32[]{:S(2)}) collective-permute-start(bf16[16,56,128]{2,1,0:T(8,128)(2,1)S(1)} %pad_maximum_fusion), channel_id=1, source_target_pairs={{0,16},{16,0},{32,48},{48,32},{64,80},{80,64},{96,112},{112,96},{1... | collective-permute-start | bytes 688136 | tf_op jit(solution)/shard_map/ppermute | solution.py:244
  37.4 4.8 %collective-permute-start = (bf16[16,40,128]{2,1,0:T(8,128)(2,1)S(1)}, bf16[16,40,128]{2,1,0:T(8,128)(2,1)S(1)}, u32[]{:S(2)}, u32[]{:S(2)}) collective-permute-start(bf16[16,40,128]{2,1,0:T(8,128)(2,1)S(1)} %get-tuple-element.7), channel_id=1, source_target_pairs={{0,2},{2,4},{4,6},{6,8},{8,10},{10,12},{12,14},{14,30},{30,28},{28... | collective-permute-start | bytes 491528 | tf_op jit(solution)/shard_map/ppermute | solution.py:251
  37.5 6.6 %collective-permute-start.1 = (bf16[16,40,128]{2,1,0:T(8,128)(2,1)S(1)}, bf16[16,40,128]{2,1,0:T(8,128)(2,1)S(1)}, u32[]{:S(2)}, u32[]{:S(2)}) collective-permute-start(bf16[16,40,128]{2,1,0:T(8,128)(2,1)S(1)} %get-tuple-element.6), channel_id=1, source_target_pairs={{2,0},{4,2},{6,4},{8,6},{10,8},{12,10},{14,12},{30,14},{28,30},{26... | collective-permute-start | bytes 491528 | tf_op jit(solution)/shard_map/ppermute | solution.py:252
